TPU v7x, 256 devices: a whole 4x4x8 slice. The times are simulated.
256 devices in a mesh: blk: 16 (over z_lo, x, core), eng: 16 (over z_hi, y).
Axes of the slice: x: 4, y: 4, z: 8 (z_hi: 4, z_lo: 2; z = z_hi * 2 + z_lo), core: 2. Of those that a mesh axis runs over, the one named last changes fastest.
Arguments:
- g_lesser: bfloat16 [64, 16, 2, 256, 256], P('eng', 'blk'), may hold values from -6 to 6
- g_greater: bfloat16 [64, 16, 2, 256, 256], P('eng', 'blk'), may hold values from -6 to 6
- coulomb: bfloat16 [16, 2, 256, 256], P('blk'), may hold values from -0.21875 to 0.21875
- coupling: int32 [16], P('blk'), may hold values 0 or 1
- lag_slots: int32 [64], replicated, may hold values from 0 to 63
Outputs:
- sigma_lesser: bfloat16 [64, 16, 2, 256, 256], P('eng', 'blk')
- sigma_greater: bfloat16 [64, 16, 2, 256, 256], P('eng', 'blk')
Inputs may be any that keep to these rules, and one draw needn't show every extreme that they name: `lag_slots`: offsets may repeat across slots.
All inputs are finite; a program needn't handle non-finite values. No bound on the sum of `coupling` on one device may be relied on, other than what follows from the above.
Results may differ from a plain program's by a relative error of at most 0.0065.
Values may be sent and summed in bfloat16 or wider, within the bound.
No kernel may reach another device: no remote copies, remote signals or barrier semaphores. Data moves between devices by JAX's collectives and lax.ppermute only.
A program may use at most 128 MiB of HBM per device.

v0:
```python
import math

import jax
import jax.numpy as jnp
from jax import lax
from jax.sharding import PartitionSpec as P


def sent_together(arrays, axis, split_dim, concat_dim, along):
    ends, at = ([], 0)
    for a in arrays[:-1]:
        at += a.shape[along]
        ends.append(at)
    both = jnp.concatenate(arrays, axis=along)
    return tuple(
        jnp.split(
            lax.all_to_all(both, axis, split_axis=split_dim, concat_axis=concat_dim, tiled=True),
            ends,
            axis=along,
        )
    )


def padded_2(array, sides, width):
    for axis, dim in sides:
        devices, length = (lax.axis_size(axis), array.shape[dim])
        up = [(i, (i + 1) % devices) for i in range(devices - 1)]
        down = [(j, i) for i, j in up]
        last = lax.slice_in_dim(array, length - width, length, axis=dim)
        leading = lax.slice_in_dim(array, 0, width, axis=dim)
        before = lax.ppermute(last, axis, up)
        after = lax.ppermute(leading, axis, down)
        array = jnp.concatenate([before, array, after], axis=dim)
    return array


def product(einsum_form, left_side, right_side):
    return jnp.einsum(einsum_form, left_side, right_side, preferred_element_type=jnp.float32)


def screen(pad_p, pad_v):
    row_count = pad_v.shape[0] - 2
    v_diag_zero = pad_v[1 : row_count + 1, 0]
    v_diag_plus = pad_v[2:, 0]
    v_up_minus = pad_v[:row_count, 1]
    v_up_zero = pad_v[1 : row_count + 1, 1]
    v_up_plus = pad_v[2:, 1]
    p_diag_minus = pad_p[:, :row_count, 0]
    p_diag_zero = pad_p[:, 1 : row_count + 1, 0]
    p_diag_plus = pad_p[:, 2:, 0]
    p_up_minus = pad_p[:, :row_count, 1]
    p_up_zero = pad_p[:, 1 : row_count + 1, 1]
    p_up_plus = pad_p[:, 2:, 1]
    q_minus = (
        product("rba,krbc->krac", v_up_minus, p_diag_minus)
        + product("rab,krcb->krac", v_diag_zero, p_up_minus)
    ).astype(jnp.bfloat16)
    q_zero = (
        product("rba,krbc->krac", v_up_minus, p_up_minus)
        + product("rab,krbc->krac", v_diag_zero, p_diag_zero)
        + product("rab,krcb->krac", v_up_zero, p_up_zero)
    ).astype(jnp.bfloat16)
    q_plus = (
        product("rab,krbc->krac", v_diag_zero, p_up_zero)
        + product("rab,krbc->krac", v_up_zero, p_diag_plus)
    ).astype(jnp.bfloat16)
    q_far = product("rab,krbc->krac", v_up_zero, p_up_plus).astype(jnp.bfloat16)
    w_diag = (
        product("krab,rbc->krac", q_minus, v_up_minus)
        + product("krab,rbc->krac", q_zero, v_diag_zero)
        + product("krab,rcb->krac", q_plus, v_up_zero)
    )
    w_upper = (
        product("krab,rbc->krac", q_zero, v_up_zero)
        + product("krab,rbc->krac", q_plus, v_diag_plus)
        + product("krab,rcb->krac", q_far, v_up_plus)
    )
    return jnp.stack([w_diag, w_upper], axis=2).astype(jnp.bfloat16)


def tables(row_ids, column_ids, energies):
    phase_ids = row_ids[:, None] * column_ids[None, :] % energies
    angles = phase_ids.astype(jnp.float32) * (2.0 * math.pi / energies)
    return (jnp.cos(angles), jnp.sin(angles))


def matmul(lookup_table, values_in):
    return jnp.dot(
        lookup_table, values_in, precision=lax.Precision.HIGHEST, preferred_element_type=jnp.float32
    )


def correlate_pair(lesser, greater, lag_slots):
    energies = lesser.shape[0]
    layout = lesser.shape
    norm_factor = energies ** (-0.5)
    slot_ids = jnp.arange(energies, dtype=jnp.int32)
    cos_tab, sin_tab = tables(slot_ids, slot_ids, energies)
    cos_lag, sin_lag = tables(lag_slots, slot_ids, energies)
    flat_lesser = lesser.reshape(energies, -1).astype(jnp.float32)
    flat_greater = greater.reshape(energies, -1).astype(jnp.float32)
    lesser_re = matmul(cos_tab, flat_lesser)
    lesser_im = -matmul(sin_tab, flat_lesser)
    greater_re = matmul(cos_tab, flat_greater)
    greater_im = -matmul(sin_tab, flat_greater)
    cross_re = lesser_re * greater_re + lesser_im * greater_im
    cross_im = lesser_im * greater_re - lesser_re * greater_im
    back_re = matmul(cos_lag, cross_re)
    back_im = matmul(sin_lag, cross_im)
    factor = norm_factor / energies
    polar_lesser = ((back_re - back_im) * factor).astype(jnp.bfloat16).reshape(layout)
    polar_greater = ((back_re + back_im) * factor).astype(jnp.bfloat16).reshape(layout)
    return (polar_lesser, polar_greater)


def convolve_pair(green_lesser, green_greater, w_lesser, w_greater, lag_slots):
    energies = green_lesser.shape[0]
    layout = green_lesser.shape
    norm_factor = energies ** (-0.5)
    slot_ids = jnp.arange(energies, dtype=jnp.int32)
    cos_tab, sin_tab = tables(slot_ids, slot_ids, energies)
    cos_lag, sin_lag = tables(slot_ids, lag_slots, energies)

    def convolve_kind(green_part, screened_part):
        flat_green = green_part.reshape(energies, -1).astype(jnp.float32)
        flat_screen = screened_part.reshape(energies, -1).astype(jnp.float32)
        green_re = matmul(cos_tab, flat_green)
        green_im = -matmul(sin_tab, flat_green)
        screen_re = matmul(cos_lag, flat_screen)
        screen_im = -matmul(sin_lag, flat_screen)
        joint_re = green_re * screen_re - green_im * screen_im
        joint_im = green_re * screen_im + green_im * screen_re
        result = matmul(cos_tab, joint_re) - matmul(sin_tab, joint_im)
        return (result * (norm_factor / energies)).astype(jnp.bfloat16).reshape(layout)

    return (convolve_kind(green_lesser, w_lesser), convolve_kind(green_greater, w_greater))


def on_device(g_lesser, g_greater, coulomb, coupling, lag_slots):
    own_energies = g_lesser.shape[0]
    row_count = g_lesser.shape[1]
    el_lesser, el_greater = sent_together((g_lesser, g_greater), "eng", 3, 0, 1)
    polar_lesser, polar_greater = correlate_pair(el_lesser, el_greater, lag_slots)
    polar_lesser, polar_greater = sent_together((polar_lesser, polar_greater), "eng", 0, 3, 1)
    row_ids = lax.axis_index("blk") * row_count + jnp.arange(row_count, dtype=jnp.int32)
    all_rows = row_count * lax.axis_size("blk")
    kept_links = (coupling * (row_ids < all_rows - 1).astype(jnp.int32)).astype(jnp.bfloat16)
    v_both = jnp.stack([coulomb[:, 0], coulomb[:, 1] * kept_links[:, None, None]], axis=1)
    stacked = jnp.concatenate([polar_lesser, polar_greater, v_both[None]], axis=0)
    padded = padded_2(stacked, (("blk", 1),), 1)
    screened = screen(padded[: 2 * own_energies], padded[2 * own_energies])
    w_lesser = screened[:own_energies]
    w_greater = screened[own_energies:]
    w_el_lesser, w_el_greater = sent_together((w_lesser, w_greater), "eng", 3, 0, 1)
    green_lesser, green_greater = (el_lesser, el_greater)
    self_lesser, self_greater = convolve_pair(
        green_lesser, green_greater, w_el_lesser, w_el_greater, lag_slots
    )
    sigma_lesser, sigma_greater = sent_together((self_lesser, self_greater), "eng", 0, 3, 1)
    return (sigma_lesser, sigma_greater)


def solution(mesh):
    return jax.shard_map(
        on_device,
        mesh=mesh,
        in_specs=(
            P("eng", "blk", None, None, None),
            P("eng", "blk", None, None, None),
            P("blk", None, None, None),
            P("blk"),
            P(),
        ),
        out_specs=(P("eng", "blk", None, None, None), P("eng", "blk", None, None, None)),
        check_vma=False,
    )
```

profile of v0, /device:TPU:66, one launch (start us, length us, event | category | flops | bytes accessed | tf_op | source)
XLA Modules:
  0.0 330.0 jit_solution(6922993020544334369)
XLA Ops:
  0.6 2.4 copy.67
  4.1 2.7 pad_maximum_fusion.2
  6.8 61.7 %all_to_all.72 = bf16[4,2,2,256,256]{4,2,1,0,3:T(2,128)(2,1)S(1)} all-to-all(bf16[4,2,2,256,256]{4,2,1,0,3:T(2,128)(2,1)S(1)} %pad_maximum_fusion.2), channel_id=1, replica_groups=mesh['blk'=16,'eng'=16] {'eng'}, dimensions={3} | all-to-all | bytes 4194304 | tf_op jit(solution)/shard_map/all_to_all | solution.py:17
  75.5 2.4 fusion.21
  77.9 2.5 multiply_convert_fusion.1
  82.4 5.6 %all-to-all-start.1 = ((bf16[64,2,2,16,256]{4,3,2,1,0:T(8,128)(2,1)}), bf16[64,2,2,16,256]{4,3,2,1,0:T(8,128)(2,1)}, u32[]{:S(2)}, u32[]{:S(2)}) async-start(bf16[64,2,2,16,256]{4,3,2,1,0:T(8,128)(2,1)} %pad_maximum_fusion.3), calls=%async_computation.1 | async-start | bytes 4194304 | tf_op jit(solution)/shard_map/all_to_all | solution.py:17
  88.7 43.4 %all-to-all-done.1 = bf16[64,2,2,16,256]{4,3,2,1,0:T(8,128)(2,1)} async-done(((bf16[64,2,2,16,256]{4,3,2,1,0:T(8,128)(2,1)}), bf16[64,2,2,16,256]{4,3,2,1,0:T(8,128)(2,1)}, u32[]{:S(2)}, u32[]{:S(2)}) %all-to-all-start.1) | async-done | bytes 2097184 | tf_op jit(solution)/shard_map/all_to_all | solution.py:17
  132.1 1.8 copy.72
  134.4 1.9 collective-permute-start.1
  136.3 2.4 collective-permute-start
  138.7 23.9 %collective-permute-done.1 = bf16[9,1,2,256,256]{4,3,2,1,0:T(8,128)(2,1)S(1)} collective-permute-done((bf16[9,1,2,256,256]{4,3,2,1,0:T(8,128)(2,1)S(1)}, bf16[9,1,2,256,256]{4,3,2,1,0:T(8,128)(2,1)S(1)}, u32[]{:S(2)}, u32[]{:S(2)}) %collective-permute-start.1) | collective-permute-done | bytes 2359328 | tf_op jit(solution)/shard_map/ppermute | solution.py:32
  162.7 3.8 %collective-permute-done = bf16[9,1,2,256,256]{4,3,2,1,0:T(8,128)(2,1)S(1)} collective-permute-done((bf16[9,1,2,256,256]{4,3,2,1,0:T(8,128)(2,1)S(1)}, bf16[9,1,2,256,256]{4,3,2,1,0:T(8,128)(2,1)S(1)}, u32[]{:S(2)}, u32[]{:S(2)}) %collective-permute-start) | collective-permute-done | bytes 2359328 | tf_op jit(solution)/shard_map/ppermute | solution.py:31
  168.6 1.9 fusion.54
  175.5 1.8 fusion.46
  177.3 4.4 %fusion.36 = f32[256,8,256]{2,0,1:T(8,128)} fusion(f32[8,256,256]{2,1,0:T(8,128)} %fusion.46, bf16[9,1,2,256,256]{4,3,2,1,0:T(8,128)(2,1)} %copy-done.6, bf16[3,2,256,256]{3,2,1,0:T(8,128)(2,1)S(1)} %fusion.47), kind=kOutput, calls=%fused_computation.55 | convolution fusion | flops 537919488 | bytes 5505024 | tf_op jit(solution)/shard_map/krab,rbc->krac/dot_general | solution.py:38
  181.7 3.0 fusion.38
  184.8 4.5 %fusion.39 = bf16[8,1,1,256,256]{3,4,0,2,1:T(8,128)(2,1)} fusion(f32[256,8,256]{2,0,1:T(8,128)} %fusion.54, f32[256,8,256]{2,0,1:T(8,128)} %fusion.52, bf16[9,1,2,256,256]{4,3,2,1,0:T(8,128)(2,1)} %copy-done.10, bf16[3,2,256,256]{3,2,1,0:T(8,128)(2,1)} %copy-done.9), kind=kOutput, calls=%fused_computation.58 | convolution fusion | flops 538968064 | bytes 6553600 | tf_op jit(solution)/shard_map/krab,rcb->krac/dot_general | solution.py:38
  192.2 4.5 %copy.89 = bf16[4,2,2,256,256]{4,0,2,1,3:T(4,128)(2,1)} copy(bf16[4,2,2,256,256]{3,4,0,2,1:T(8,128)(2,1)} %fusion.4) | data formatting | bytes 4194304 | tf_op jit(solution)/shard_map/concatenate | solution.py:14
  196.7 48.9 %all_to_all.73 = bf16[4,2,2,256,256]{4,0,2,1,3:T(4,128)(2,1)S(1)} all-to-all(bf16[4,2,2,256,256]{4,0,2,1,3:T(4,128)(2,1)} %copy.89), channel_id=1, replica_groups=mesh['blk'=16,'eng'=16] {'eng'}, dimensions={3} | all-to-all | bytes 4194304 | tf_op jit(solution)/shard_map/all_to_all | solution.py:17
  253.2 2.1 fusion.9
  255.3 2.4 fusion.3
  259.3 2.5 fusion.17
  261.8 2.5 fusion.2
  264.8 63.2 %all_to_all.74 = bf16[64,2,2,16,256]{4,3,2,1,0:T(8,128)(2,1)S(1)} all-to-all(bf16[64,2,2,16,256]{4,3,2,1,0:T(8,128)(2,1)S(1)} %pad_maximum_fusion.4), channel_id=1, replica_groups=mesh['blk'=16,'eng'=16] {'eng'}, dimensions={0} | all-to-all | bytes 4194304 | tf_op jit(solution)/shard_map/all_to_all | solution.py:17
  (69 shorter events, 31.6 us)
Async XLA Ops:
  0.6 2.4 copy-start.11
  71.5 6.4 %copy-start.2 = (f32[64,8192]{1,0:T(8,128)}, f32[64,8192]{1,0:T(8,128)S(1)}, u32[]{:S(2)}) copy-start(f32[64,8192]{1,0:T(8,128)S(1)} %fusion.85) | copy-start | bytes 6291460
  72.6 5.3 %copy-start.4 = (f32[64,8192]{1,0:T(8,128)}, f32[64,8192]{1,0:T(8,128)S(1)}, u32[]{:S(2)}) copy-start(f32[64,8192]{1,0:T(8,128)S(1)} %fusion.79) | copy-start | bytes 6291460
  74.4 1.1 copy-start.13
  75.5 2.4 copy-start
  82.4 6.3 %copy-start.12 = (bf16[1,2,256,256]{3,2,1,0:T(8,128)(2,1)S(1)}, bf16[1,2,256,256]{3,2,1,0:T(8,128)(2,1)}, u32[]{:S(2)}) copy-start(bf16[1,2,256,256]{3,2,1,0:T(8,128)(2,1)} %param.7) | copy-start | bytes 786436
  82.4 49.7 %all-to-all-start.1 = ((bf16[64,2,2,16,256]{4,3,2,1,0:T(8,128)(2,1)}), bf16[64,2,2,16,256]{4,3,2,1,0:T(8,128)(2,1)}, u32[]{:S(2)}, u32[]{:S(2)}) async-start(bf16[64,2,2,16,256]{4,3,2,1,0:T(8,128)(2,1)} %pad_maximum_fusion.3), calls=%async_computation.1 | async-start | bytes 4194304 | tf_op jit(solution)/shard_map/all_to_all | solution.py:17
  134.4 28.3 %collective-permute-start.1 = (bf16[9,1,2,256,256]{4,3,2,1,0:T(8,128)(2,1)S(1)}, bf16[9,1,2,256,256]{4,3,2,1,0:T(8,128)(2,1)S(1)}, u32[]{:S(2)}, u32[]{:S(2)}) collective-permute-start(bf16[9,1,2,256,256]{4,3,2,1,0:T(8,128)(2,1)S(1)} %pad_maximum_fusion), channel_id=1, source_target_pairs={{16,0},{32,16},{48,32},{64,48},{80,64},{96,80},{112,96},{128,112},... | collective-permute-start | bytes 7077896 | tf_op jit(solution)/shard_map/ppermute | solution.py:32
  136.3 30.2 %collective-permute-start = (bf16[9,1,2,256,256]{4,3,2,1,0:T(8,128)(2,1)S(1)}, bf16[9,1,2,256,256]{4,3,2,1,0:T(8,128)(2,1)S(1)}, u32[]{:S(2)}, u32[]{:S(2)}) collective-permute-start(bf16[9,1,2,256,256]{4,3,2,1,0:T(8,128)(2,1)S(1)} %pad_maximum_fusion), channel_id=1, source_target_pairs={{0,16},{16,32},{32,48},{48,64},{64,80},{80,96},{96,112},{112,128},... | collective-permute-start | bytes 7077896 | tf_op jit(solution)/shard_map/ppermute | solution.py:31
  162.7 9.6 %copy-start.10 = (bf16[9,1,2,256,256]{4,3,2,1,0:T(8,128)(2,1)}, bf16[9,1,2,256,256]{4,3,2,1,0:T(8,128)(2,1)S(1)}, u32[]{:S(2)}) copy-start(bf16[9,1,2,256,256]{4,3,2,1,0:T(8,128)(2,1)S(1)} %collective-permute-done.1) | copy-start | bytes 7077892
  166.5 9.0 %copy-start.6 = (bf16[9,1,2,256,256]{4,3,2,1,0:T(8,128)(2,1)}, bf16[9,1,2,256,256]{4,3,2,1,0:T(8,128)(2,1)S(1)}, u32[]{:S(2)}) copy-start(bf16[9,1,2,256,256]{4,3,2,1,0:T(8,128)(2,1)S(1)} %collective-permute-done) | copy-start | bytes 7077892
  166.6 10.7 %copy-start.9 = (bf16[3,2,256,256]{3,2,1,0:T(8,128)(2,1)}, bf16[3,2,256,256]{3,2,1,0:T(8,128)(2,1)S(1)}, u32[]{:S(2)}) copy-start(bf16[3,2,256,256]{3,2,1,0:T(8,128)(2,1)S(1)} %fusion.47) | copy-start | bytes 2359300
  172.7 1.0 copy-start.8
  189.3 1.4 copy-start.7
  250.4 2.2 copy-start.5
  251.5 1.7 copy-start.3
  257.7 1.6 copy-start.1
where the time goes:
time: 335 us; the launch traced here: 330 us
  blocking collectives  174 us (52%)
  waiting for transfers between devices  71.1 us (21%)
  matrix products  44.8 us (13%)
  local copies, waits for them, and re-layouts  20.7 us (6%)
  starting transfers between devices  9.95 us (3%)
  other arithmetic  7.58 us (2%)
    all_to_all x3, blocking collectives, sent_together(): lax.all_to_all(both, axis, split_axis=split_dim, concat_axis=concat_dim,...  174 us
    all_to_all x1, waiting for transfers between devices, sent_together(): lax.all_to_all(both, axis, split_axis=split_dim, concat_axis=concat_dim,...  43.4 us
    ppermute x1, waiting for transfers between devices, padded_2(): after = lax.ppermute(leading, axis, down)  23.9 us
    dot_general x14, matrix products, matmul(): jnp.dot(lookup_table, values_in, precision=lax.Precision.HIGHEST, preferr...  23.1 us
    dot_general x12, matrix products, product(): jnp.einsum(einsum_form, left_side, right_side, preferred_element_type=jnp...  21.7 us
    unnamed x38, local copies, waits for them, and re-layouts  10.1 us
  transfers between devices with their start and end apart: 3, of which 3 were waited for; matrix products, arithmetic and copies ran while one was open for 0% of the time, Pallas kernels for 0%

commit v1 on v0

v1 whole, which is shorter than its diff:
```python
import jax
import jax.numpy as jnp
import numpy as np
from jax import lax
from jax.experimental import pallas as pl
from jax.experimental.pallas import tpu as pltpu
from jax.sharding import PartitionSpec as P

BF = jnp.bfloat16
F32 = jnp.float32


def real_tables(n):
    h = n // 2
    f = np.arange(h)[:, None]
    k = np.arange(n)[None, :]
    ang = 2.0 * np.pi * (f * k % n) / n
    re = np.cos(ang)
    im = -np.sin(ang)
    im[0] = np.cos(np.pi * k[0])
    fwd = np.concatenate([re, im], 0)
    w = np.full((2 * h, 1), 2.0)
    w[0] = 1.0
    w[h] = 1.0
    inv = (fwd * w).T / n
    return fwd.astype(np.float32), inv.astype(np.float32)


def split2(x):
    hi = x.astype(BF)
    lo = (x - hi.astype(F32)).astype(BF)
    return hi, lo


def dot(a, b):
    return jnp.dot(a, b, preferred_element_type=F32)


def forward(tab, x):
    n = tab.shape[0]
    hi, lo = split2(tab)
    both = dot(jnp.concatenate([hi, lo], 0), x)
    return both[:n] + both[n:]


def backward(tab, re, im):
    hi, lo = split2(tab)
    xh, xl = split2(jnp.concatenate([re, im], 0))
    return dot(jnp.concatenate([hi, hi, lo], 1), jnp.concatenate([xh, xl, xh], 0))


def corr_kernel(fwd_ref, inv_ref, l_ref, g_ref, c_ref):
    h = fwd_ref.shape[0] // 2
    fl = forward(fwd_ref[...], l_ref[...])
    fg = forward(fwd_ref[...], g_ref[...])
    lr, li, gr, gi = fl[:h], fl[h:], fg[:h], fg[h:]
    first = lax.broadcasted_iota(jnp.int32, lr.shape, 0) == 0
    rr, ii = lr * gr, li * gi
    re = rr + jnp.where(first, 0.0, ii)
    im = jnp.where(first, ii, li * gr - lr * gi)
    c_ref[...] = backward(inv_ref[...], re, im).astype(c_ref.dtype)


def conv_kernel(fwd_ref, lag_ref, inv_ref, g_ref, d_ref, s_ref):
    h = fwd_ref.shape[0] // 2
    fg = forward(fwd_ref[...], g_ref[...])
    fd = forward(lag_ref[0], d_ref[...])
    gr, gi, dr, di = fg[:h], fg[h:], fd[:h], fd[h:]
    first = lax.broadcasted_iota(jnp.int32, gr.shape, 0) == 0
    rr, ii = gr * dr, gi * di
    re = rr - jnp.where(first, 0.0, ii)
    im = jnp.where(first, ii, gr * di + gi * dr)
    s_ref[...] = backward(inv_ref[...], re, im).astype(s_ref.dtype)


def dot_t(a, b):
    return lax.dot_general(a, b, (((1,), (1,)), ((), ())), preferred_element_type=F32)


def t_dot(a, b):
    return lax.dot_general(a, b, (((0,), (0,)), ((), ())), preferred_element_type=F32)


def screen_kernel(vm_ref, v0_ref, vp_ref, pm_ref, p0_ref, pp_ref, w_ref):
    def block(ref, j):
        x = ref[:, j]
        return x.reshape(x.shape[0] * x.shape[1], x.shape[2])

    vum, vd0, vu0 = block(vm_ref, 1), block(v0_ref, 0), block(v0_ref, 1)
    vdp, vup = block(vp_ref, 0), block(vp_ref, 1)
    dm, um = block(pm_ref, 0), block(pm_ref, 1)
    d0, u0 = block(p0_ref, 0), block(p0_ref, 1)
    dp, up = block(pp_ref, 0), block(pp_ref, 1)
    q_minus = (t_dot(vum, dm) + dot_t(vd0, um)).astype(BF)
    q_zero = (t_dot(vum, um) + dot(vd0, d0) + dot_t(vu0, u0)).astype(BF)
    q_plus = (dot(vd0, u0) + dot(vu0, dp)).astype(BF)
    q_far = dot(vu0, up).astype(BF)
    w_diag = dot(q_minus, vum) + dot(q_zero, vd0) + dot_t(q_plus, vu0)
    w_up = dot(q_zero, vu0) + dot(q_plus, vdp) + dot_t(q_far, vup)
    shape = w_ref.shape[:1] + w_ref.shape[2:]
    w_ref[:, 0] = w_diag.astype(w_ref.dtype).reshape(shape)
    w_ref[:, 1] = w_up.astype(w_ref.dtype).reshape(shape)


def full(a):
    return pl.BlockSpec(a.shape, lambda *_: (0,) * a.ndim)


def correlate(fwd, inv, flat, tile):
    n, both = flat.shape
    tiles = both // 2 // tile
    return pl.pallas_call(
        corr_kernel,
        grid=(tiles,),
        in_specs=[
            full(fwd),
            full(inv),
            pl.BlockSpec((n, tile), lambda j: (0, j)),
            pl.BlockSpec((n, tile), lambda j: (0, j + tiles)),
        ],
        out_specs=pl.BlockSpec((n, tile), lambda j: (0, j)),
        out_shape=jax.ShapeDtypeStruct((n, both // 2), BF),
        name="corr",
    )(fwd, inv, flat, flat)


def convolve(fwd, lag_tabs, inv, flat, d, tile):
    n, both = flat.shape
    tiles = both // 2 // tile
    return pl.pallas_call(
        conv_kernel,
        grid=(2, tiles),
        in_specs=[
            full(fwd),
            pl.BlockSpec((1,) + lag_tabs.shape[1:], lambda s, j: (s, 0, 0)),
            full(inv),
            pl.BlockSpec((n, tile), lambda s, j: (0, s * tiles + j)),
            pl.BlockSpec((n, tile), lambda s, j: (0, j)),
        ],
        out_specs=pl.BlockSpec((n, tile), lambda s, j: (0, s * tiles + j)),
        out_shape=jax.ShapeDtypeStruct((n, both), BF),
        name="conv",
    )(fwd, lag_tabs, inv, flat, d)


def screen(stack, before, after, count):
    r, _, t, s, b = stack.shape
    one = (r, None, t, s, b)

    def at(k):
        return pl.BlockSpec(one, lambda j: (0, k, 0, 0, 0))

    def each():
        return pl.BlockSpec(one, lambda j: (0, j, 0, 0, 0))

    return pl.pallas_call(
        screen_kernel,
        grid=(count,),
        in_specs=[at(count), at(count), at(count), each(), each(), each()],
        out_specs=each(),
        out_shape=jax.ShapeDtypeStruct((r, count, t, s, b), BF),
        name="screen",
    )(before, stack, after, before, stack, after)


def exchange(x):
    return lax.all_to_all(x, "eng", split_axis=0, concat_axis=0, tiled=True)


def on_device(g_lesser, g_greater, coulomb, coupling, lag_slots):
    parts = lax.axis_size("eng")
    blocks = lax.axis_size("blk")
    own, _, two, bs, _ = g_lesser.shape
    energies = own * parts
    slab = bs // parts
    norm = energies ** (-0.5)
    fwd_np, inv_np = real_tables(energies)
    fwd = jnp.asarray(fwd_np)
    inv = jnp.asarray(inv_np * np.float32(norm))
    back_ids = (-np.arange(energies)) % energies
    ids = jnp.arange(energies, dtype=jnp.int32)
    cnt = jnp.sum((lag_slots[:, None] == ids[None, :]).astype(F32), axis=0)
    cnt_neg = jnp.sum((lag_slots[:, None] == jnp.asarray(back_ids, jnp.int32)[None, :]).astype(F32), axis=0)
    lag_tabs = jnp.stack([fwd * cnt[None], jnp.asarray(fwd_np[:, back_ids]) * cnt_neg[None]])

    both = jnp.stack([g_lesser[:, 0], g_greater[:, 0]], axis=1)
    both = both.reshape(own, 2, two, parts, slab, bs).transpose(3, 0, 1, 2, 4, 5)
    el = exchange(both).reshape(energies, 2 * two * slab * bs)
    tile = two * slab * bs // 4
    c = correlate(fwd, inv, el, tile)
    p = exchange(c.reshape(parts, own, two, slab, bs))

    row = lax.axis_index("blk")
    kept = (coupling[0] * (row < blocks - 1).astype(jnp.int32)).astype(BF)
    v_both = jnp.stack([coulomb[0, 0], coulomb[0, 1] * kept], axis=0)
    v_both = v_both.reshape(two, parts, 1, slab, bs).transpose(1, 2, 0, 3, 4)
    stack = jnp.concatenate([p, v_both], axis=1)
    ups = [(i, i + 1) for i in range(blocks - 1)]
    before = lax.ppermute(stack, "blk", ups)
    after = lax.ppermute(stack, "blk", [(j, i) for i, j in ups])
    w = screen(stack, before, after, own)

    d = exchange(w).reshape(energies, two * slab * bs)
    s = convolve(fwd, lag_tabs, inv, el, d, tile)
    s = exchange(s.reshape(parts, own, 2, two, slab, bs))
    s = s.transpose(1, 2, 3, 0, 4, 5).reshape(own, 2, 1, two, bs, bs)
    return (s[:, 0], s[:, 1])


def solution(mesh):
    spec = P("eng", "blk", None, None, None)
    return jax.shard_map(
        on_device,
        mesh=mesh,
        in_specs=(spec, spec, P("blk", None, None, None), P("blk"), P()),
        out_specs=(spec, spec),
        check_vma=False,
    )
```

time: 335 us -> 240 us (0.72)
  blocking collectives: 174 us -> 118 us
  matrix products: 44.8 us -> 0 us
  Pallas kernels: 0 us -> 18.7 us
  local copies, waits for them, and re-layouts: 20.7 us -> 10.2 us
  starting transfers between devices: 9.95 us -> 18 us
  other arithmetic: 7.58 us -> 2.64 us
    all_to_all x3 -> x2, blocking collectives: 174 us -> 118 us  [exchange(): return lax.all_to_all(x, 'eng', split_axis=0, concat_axis=0, tiled=True)]
    dot_general x26 -> x0, matrix products: 44.8 us -> none  [the longest x14 23.1 us: matmul(): jnp.dot(lookup_table, values_in, precision=lax.Precision.HIGHEST, preferr...]
    pallas_call x0 -> x3, Pallas kernels: none -> 18.7 us  [the longest x1 8.4 us: convolve(): pl.pallas_call(conv_kernel, grid=(2, tiles), in_specs=[full(fwd), pl.Bloc...]
    ppermute x2, waiting for transfers between devices: 27.7 us -> 15.1 us  [the longest x1 13.3 us: on_device(): before = lax.ppermute(stack, 'blk', ups)]
    all_to_all x1 -> x2, waiting for transfers between devices: 43.4 us -> 53.3 us  [exchange(): return lax.all_to_all(x, 'eng', split_axis=0, concat_axis=0, tiled=True)]
    all_to_all x1 -> x2, starting transfers between devices: 5.63 us -> 12.4 us  [exchange(): return lax.all_to_all(x, 'eng', split_axis=0, concat_axis=0, tiled=True)]
    concatenate x5 -> x1, other arithmetic: 6.22 us -> 0.12 us  [on_device(): stack = jnp.concatenate([p, v_both], axis=1)]
    unnamed x38 -> x16, local copies, waits for them, and re-layouts: 10.1 us -> 4.66 us
  transfers between devices with their start and end apart: 3 -> 4, of which waited for: 3 -> 4; matrix products, arithmetic and copies ran while one was open for 0% -> 0% of each run, Pallas kernels for 0% -> 0%
where the time goes in v1:
time: 240 us; the launch traced here: 238 us
  blocking collectives  118 us (49%)
  waiting for transfers between devices  68.4 us (29%)
  Pallas kernels  18.7 us (8%)
  starting transfers between devices  18 us (8%)
  local copies, waits for them, and re-layouts  10.2 us (4%)
  other arithmetic  2.64 us (1%)
    all_to_all x2, blocking collectives, exchange(): return lax.all_to_all(x, 'eng', split_axis=0, concat_axis=0, tiled=True)  118 us
    all_to_all x2, waiting for transfers between devices, exchange(): return lax.all_to_all(x, 'eng', split_axis=0, concat_axis=0, tiled=True)  53.3 us
    ppermute x1, waiting for transfers between devices, on_device(): before = lax.ppermute(stack, 'blk', ups)  13.3 us
    all_to_all x2, starting transfers between devices, exchange(): return lax.all_to_all(x, 'eng', split_axis=0, concat_axis=0, tiled=True)  12.4 us
    pallas_call x1, Pallas kernels, convolve(): pl.pallas_call(conv_kernel, grid=(2, tiles), in_specs=[full(fwd), pl.Bloc...  8.4 us
    pallas_call x1, Pallas kernels, screen(): pl.pallas_call(screen_kernel, grid=(count,), in_specs=[at(count), at(coun...  5.56 us
  transfers between devices with their start and end apart: 4, of which 4 were waited for; matrix products, arithmetic and copies ran while one was open for 0% of the time, Pallas kernels for 0%

profile of v1, /device:TPU:66, one launch (start us, length us, event | category | flops | bytes accessed | tf_op | source)
XLA Modules:
  0.0 237.5 jit_solution(12138603674183504418)
XLA Ops:
  0.6 1.7 pad_maximum_fusion
  2.4 0.3 copy.18
  2.7 61.2 %all_to_all.20 = bf16[16,4,2,2,16,256]{5,4,3,2,1,0:T(8,128)(2,1)S(1)} all-to-all(bf16[16,4,2,2,16,256]{5,4,3,2,1,0:T(8,128)(2,1)S(1)} %bitcast.31), channel_id=1, replica_groups=mesh['blk'=16,'eng'=16] {'eng'}, dimensions={0} | all-to-all | bytes 4194304 | tf_op jit(solution)/shard_map/all_to_all | solution.py:167
  63.8 2.3 reshape.44.l_ref.g_ref
  66.2 4.8 %corr.1 = bf16[64,8192]{1,0:T(8,128)(2,1)} custom-call(f32[64,64]{1,0:T(8,128)} %constant.19.clone.fwd_ref, f32[64,64]{1,0:T(8,128)} %constant.20.clone.inv_ref, bf16[64,16384]{1,0:T(8,128)(2,1)} %reshape.44.l_ref.g_ref, bf16[64,16384]{1,0:T(8,128)(2,1)} %reshape.44.l_ref.g_ref), custom_call_target="tpu_custom_call" | custom-call | tf_op jit(solution)/shard_map/corr/pallas_call | solution.py:112
  70.9 2.5 %copy.15 = bf16[8,8,32,256]{3,2,1,0:T(8,128)(2,1)} copy(bf16[8,8,32,256]{3,1,2,0:T(8,128)(2,1)} %bitcast.36) | data formatting | bytes 2097152
  73.4 5.5 %all-to-all-start.1 = ((bf16[16,4,2,16,256]{4,3,2,1,0:T(8,128)(2,1)}), bf16[16,4,2,16,256]{4,3,2,1,0:T(8,128)(2,1)S(1)}, u32[]{:S(2)}, u32[]{:S(2)}) async-start(bf16[16,4,2,16,256]{4,3,2,1,0:T(8,128)(2,1)} %bitcast.15), calls=%async_computation.1 | async-start | bytes 2097152 | tf_op jit(solution)/shard_map/all_to_all | solution.py:167
  79.6 26.2 %all-to-all-done.1 = bf16[16,4,2,16,256]{4,3,2,1,0:T(8,128)(2,1)S(1)} async-done(((bf16[16,4,2,16,256]{4,3,2,1,0:T(8,128)(2,1)}), bf16[16,4,2,16,256]{4,3,2,1,0:T(8,128)(2,1)S(1)}, u32[]{:S(2)}, u32[]{:S(2)}) %all-to-all-start.1) | async-done | bytes 1048608 | tf_op jit(solution)/shard_map/all_to_all | solution.py:167
  105.8 0.1 pad_maximum_fusion.1.v0_ref.p0_ref
  105.9 1.9 collective-permute-start
  107.9 3.6 %collective-permute-start.1 = (bf16[16,5,2,16,256]{4,3,2,1,0:T(8,128)(2,1)S(1)}, bf16[16,5,2,16,256]{4,3,2,1,0:T(8,128)(2,1)}, u32[]{:S(2)}, u32[]{:S(2)}) collective-permute-start(bf16[16,5,2,16,256]{4,3,2,1,0:T(8,128)(2,1)S(1)} %pad_maximum_fusion.1.v0_ref.p0_ref), channel_id=1, source_target_pairs={{16,0},{32,16},{48,32},{64,48},{80,64},{96,80},{112,96},{128,112},... | collective-permute-start | bytes 3932168 | tf_op jit(solution)/shard_map/ppermute | solution.py:200
  111.5 13.3 %collective-permute-done.vm_ref.pm_ref = bf16[16,5,2,16,256]{4,3,2,1,0:T(8,128)(2,1)S(1)} collective-permute-done((bf16[16,5,2,16,256]{4,3,2,1,0:T(8,128)(2,1)S(1)}, bf16[16,5,2,16,256]{4,3,2,1,0:T(8,128)(2,1)S(1)}, u32[]{:S(2)}, u32[]{:S(2)}) %collective-permute-start) | collective-permute-done | bytes 1310752 | tf_op jit(solution)/shard_map/ppermute | solution.py:199
  124.9 1.8 collective-permute-done.1.vp_ref.pp_ref
  126.6 5.6 %screen.1 = bf16[16,4,2,16,256]{4,3,2,1,0:T(8,128)(2,1)} custom-call(bf16[16,5,2,16,256]{4,3,2,1,0:T(8,128)(2,1)} %copy-done.1, bf16[16,5,2,16,256]{4,3,2,1,0:T(8,128)(2,1)} %copy-done, bf16[16,5,2,16,256]{4,3,2,1,0:T(8,128)(2,1)} %collective-permute-done.1.vp_ref.pp_ref, bf16[16,5,2,16,256]{4,3,2,1,0:T(8,128)(2,1)} %copy-done.1, ...), custom_call_target="tpu_custom_call" | custom-call | tf_op jit(solution)/shard_map/screen/pallas_call | solution.py:156
  132.2 6.9 %all-to-all-start.2 = ((bf16[16,4,2,16,256]{4,3,2,1,0:T(8,128)(2,1)}), bf16[16,4,2,16,256]{4,3,2,1,0:T(8,128)(2,1)S(1)}, u32[]{:S(2)}, u32[]{:S(2)}) async-start(bf16[16,4,2,16,256]{4,3,2,1,0:T(8,128)(2,1)} %screen.1), calls=%async_computation.2 | async-start | bytes 2097152 | tf_op jit(solution)/shard_map/all_to_all | solution.py:167
  139.2 0.1 convert_reduce_fusion.1
  139.3 0.6 pad_maximum_fusion.2.lag_ref
  139.9 27.2 %all-to-all-done.2 = bf16[16,4,2,16,256]{4,3,2,1,0:T(8,128)(2,1)S(1)} async-done(((bf16[16,4,2,16,256]{4,3,2,1,0:T(8,128)(2,1)}), bf16[16,4,2,16,256]{4,3,2,1,0:T(8,128)(2,1)S(1)}, u32[]{:S(2)}, u32[]{:S(2)}) %all-to-all-start.2) | async-done | bytes 1048608 | tf_op jit(solution)/shard_map/all_to_all | solution.py:167
  167.1 1.3 reshape.46.d_ref
  168.4 8.4 %conv.1 = bf16[64,16384]{1,0:T(8,128)(2,1)} custom-call(f32[64,64]{1,0:T(8,128)} %constant.19.clone.fwd_ref, f32[2,64,64]{2,1,0:T(8,128)} %pad_maximum_fusion.2.lag_ref, f32[64,64]{1,0:T(8,128)} %constant.20.clone.inv_ref, bf16[64,16384]{1,0:T(8,128)(2,1)} %reshape.44.l_ref.g_ref, bf16[64,8192]{1,0:T(8,128)(2,1)} %reshape.46.d_ref), custom_call_target="tpu_custom_call" | custom-call | tf_op jit(solution)/shard_map/conv/pallas_call | solution.py:130
  176.8 2.1 copy.16
  178.9 57.0 %all_to_all.21 = bf16[16,4,2,2,16,256]{5,4,3,2,1,0:T(8,128)(2,1)S(1)} all-to-all(bf16[16,4,2,2,16,256]{5,4,3,2,1,0:T(8,128)(2,1)S(1)} %bitcast.32), channel_id=1, replica_groups=mesh['blk'=16,'eng'=16] {'eng'}, dimensions={0} | all-to-all | bytes 4194304 | tf_op jit(solution)/shard_map/all_to_all | solution.py:167
  235.8 0.2 copy.14
  236.1 1.5 slice_bitcast_fusion
  (17 shorter events, 0.1 us)
Async XLA Ops:
  70.9 8.6 %copy-start.3 = (bf16[1,2,256,256]{3,2,1,0:T(8,128)(2,1)S(1)}, bf16[1,2,256,256]{3,2,1,0:T(8,128)(2,1)}, u32[]{:S(2)}) copy-start(bf16[1,2,256,256]{3,2,1,0:T(8,128)(2,1)} %param.11) | copy-start | bytes 786436
  73.4 32.3 %all-to-all-start.1 = ((bf16[16,4,2,16,256]{4,3,2,1,0:T(8,128)(2,1)}), bf16[16,4,2,16,256]{4,3,2,1,0:T(8,128)(2,1)S(1)}, u32[]{:S(2)}, u32[]{:S(2)}) async-start(bf16[16,4,2,16,256]{4,3,2,1,0:T(8,128)(2,1)} %bitcast.15), calls=%async_computation.1 | async-start | bytes 2097152 | tf_op jit(solution)/shard_map/all_to_all | solution.py:167
  105.9 20.7 %copy-start = (bf16[16,5,2,16,256]{4,3,2,1,0:T(8,128)(2,1)}, bf16[16,5,2,16,256]{4,3,2,1,0:T(8,128)(2,1)S(1)}, u32[]{:S(2)}) copy-start(bf16[16,5,2,16,256]{4,3,2,1,0:T(8,128)(2,1)S(1)} %pad_maximum_fusion.1.v0_ref.p0_ref) | copy-start | bytes 3932164
  105.9 18.9 %collective-permute-start = (bf16[16,5,2,16,256]{4,3,2,1,0:T(8,128)(2,1)S(1)}, bf16[16,5,2,16,256]{4,3,2,1,0:T(8,128)(2,1)S(1)}, u32[]{:S(2)}, u32[]{:S(2)}) collective-permute-start(bf16[16,5,2,16,256]{4,3,2,1,0:T(8,128)(2,1)S(1)} %pad_maximum_fusion.1.v0_ref.p0_ref), channel_id=1, source_target_pairs={{0,16},{16,32},{32,48},{48,64},{64,80},{80,96},{96,112},{112,128},... | collective-permute-start | bytes 3932168 | tf_op jit(solution)/shard_map/ppermute | solution.py:199
  107.9 18.8 %collective-permute-start.1 = (bf16[16,5,2,16,256]{4,3,2,1,0:T(8,128)(2,1)S(1)}, bf16[16,5,2,16,256]{4,3,2,1,0:T(8,128)(2,1)}, u32[]{:S(2)}, u32[]{:S(2)}) collective-permute-start(bf16[16,5,2,16,256]{4,3,2,1,0:T(8,128)(2,1)S(1)} %pad_maximum_fusion.1.v0_ref.p0_ref), channel_id=1, source_target_pairs={{16,0},{32,16},{48,32},{64,48},{80,64},{96,80},{112,96},{128,112},... | collective-permute-start | bytes 3932168 | tf_op jit(solution)/shard_map/ppermute | solution.py:200
  124.9 1.8 copy-start.1
  132.2 7.0 %copy-start.5 = (s32[64]{0:T(128)S(1)}, s32[64]{0:T(128)}, u32[]{:S(2)}) copy-start(s32[64]{0:T(128)} %param.13) | copy-start | bytes 772
  132.2 7.0 %copy-start.6 = (s32[64]{0:T(128)S(1)}, s32[64]{0:T(128)}, u32[]{:S(2)}) copy-start(s32[64]{0:T(128)} %constant.21.clone) | copy-start | bytes 772
  132.2 7.1 %copy-start.2 = (f32[64,64]{1,0:T(8,128)S(1)}, f32[64,64]{1,0:T(8,128)}, u32[]{:S(2)}) copy-start(f32[64,64]{1,0:T(8,128)} %constant.19.clone.fwd_ref) | copy-start | bytes 49156
  132.2 7.1 %copy-start.4 = (f32[64,64]{1,0:T(8,128)S(1)}, f32[64,64]{1,0:T(8,128)}, u32[]{:S(2)}) copy-start(f32[64,64]{1,0:T(8,128)} %constant.22.clone) | copy-start | bytes 49156
  132.2 34.9 %all-to-all-start.2 = ((bf16[16,4,2,16,256]{4,3,2,1,0:T(8,128)(2,1)}), bf16[16,4,2,16,256]{4,3,2,1,0:T(8,128)(2,1)S(1)}, u32[]{:S(2)}, u32[]{:S(2)}) async-start(bf16[16,4,2,16,256]{4,3,2,1,0:T(8,128)(2,1)} %screen.1), calls=%async_computation.2 | async-start | bytes 2097152 | tf_op jit(solution)/shard_map/all_to_all | solution.py:167

commit v2 on v1

v2 whole, which is shorter than its diff:
```python
import jax
import jax.numpy as jnp
import numpy as np
from jax import lax
from jax.experimental import pallas as pl
from jax.experimental.pallas import tpu as pltpu
from jax.sharding import PartitionSpec as P

BF = jnp.bfloat16
F32 = jnp.float32


def real_tables(n):
    h = n // 2
    f = np.arange(h)[:, None]
    k = np.arange(n)[None, :]
    ang = 2.0 * np.pi * (f * k % n) / n
    re = np.cos(ang)
    im = -np.sin(ang)
    im[0] = np.cos(np.pi * k[0])
    fwd = np.concatenate([re, im], 0)
    w = np.full((2 * h, 1), 2.0)
    w[0] = 1.0
    w[h] = 1.0
    inv = (fwd * w).T / n
    return fwd.astype(np.float32), inv.astype(np.float32)


def split2(x):
    hi = x.astype(BF)
    lo = (x - hi.astype(F32)).astype(BF)
    return hi, lo


def dot(a, b):
    return jnp.dot(a, b, preferred_element_type=F32)


def wide_forward(tab):
    return jnp.concatenate(split2(tab), 1)


def forward(wide, x):
    return dot(wide, jnp.concatenate([x, x], 0))


def wide_backward(tab):
    hi, lo = split2(tab)
    return jnp.concatenate([hi, hi, lo], 1)


def backward(wide, re, im):
    xh, xl = split2(jnp.concatenate([re, im], 0))
    return dot(wide, jnp.concatenate([xh, xl, xh], 0))


def corr_kernel(fwd_ref, inv_ref, x_ref, c_ref):
    h = fwd_ref.shape[0] // 2
    columns = c_ref.shape[1]
    fwd = wide_forward(fwd_ref[...])
    fl = forward(fwd, x_ref[:, :columns])
    fg = forward(fwd, x_ref[:, columns:])
    lr, li, gr, gi = fl[:h], fl[h:], fg[:h], fg[h:]
    first = lax.broadcasted_iota(jnp.int32, lr.shape, 0) == 0
    ii = li * gi
    re = lr * gr + jnp.where(first, 0.0, ii)
    im = jnp.where(first, ii, li * gr - lr * gi)
    c_ref[...] = backward(wide_backward(inv_ref[...]), re, im).astype(c_ref.dtype)


def conv_kernel(fwd_ref, lag_ref, inv_ref, g_ref, d_ref, s_ref):
    h = fwd_ref.shape[0] // 2
    columns = d_ref.shape[1]
    fwd = wide_forward(fwd_ref[...])
    inv = wide_backward(inv_ref[...])
    for kind in range(2):
        here = slice(kind * columns, (kind + 1) * columns)
        fg = forward(fwd, g_ref[:, here])
        fd = forward(wide_forward(lag_ref[kind]), d_ref[...])
        gr, gi, dr, di = fg[:h], fg[h:], fd[:h], fd[h:]
        first = lax.broadcasted_iota(jnp.int32, gr.shape, 0) == 0
        ii = gi * di
        re = gr * dr - jnp.where(first, 0.0, ii)
        im = jnp.where(first, ii, gr * di + gi * dr)
        s_ref[:, here] = backward(inv, re, im).astype(s_ref.dtype)


def screen_kernel(m_ref, z_ref, p_ref, w_ref):
    own = w_ref.shape[1]

    def block(ref, k, j):
        x = ref[:, k, j]
        return x.reshape(x.shape[0] * x.shape[1], x.shape[2])

    def rows(*xs):
        return jnp.concatenate(xs, 0)

    def cols(*xs):
        return jnp.concatenate(xs, 1)

    vum, vd0, vu0 = block(m_ref, own, 1), block(z_ref, own, 0), block(z_ref, own, 1)
    vdp, vup = block(p_ref, own, 0), block(p_ref, own, 1)
    left = cols(vum.T, vd0, vu0)
    right_diag = rows(vum, vd0, vu0.T)
    right_up = rows(vu0, vdp, vup.T)
    n = vd0.shape[0]
    shape = (w_ref.shape[0],) + w_ref.shape[3:]
    for k in range(own):
        dm, um = block(m_ref, k, 0), block(m_ref, k, 1)
        d0, u0 = block(z_ref, k, 0), block(z_ref, k, 1)
        dp, up = block(p_ref, k, 0), block(p_ref, k, 1)
        q_minus = dot(left[:, : 2 * n], rows(dm, um.T)).astype(BF)
        q_zero = dot(left, rows(um, d0, u0.T)).astype(BF)
        q_plus = dot(left[:, n:], rows(u0, dp)).astype(BF)
        q_far = dot(left[:, 2 * n :], up).astype(BF)
        w_diag = dot(cols(q_minus, q_zero, q_plus), right_diag)
        w_up = dot(cols(q_zero, q_plus, q_far), right_up)
        w_ref[:, k, 0] = w_diag.astype(w_ref.dtype).reshape(shape)
        w_ref[:, k, 1] = w_up.astype(w_ref.dtype).reshape(shape)


def local_call(kernel, out_shape, name, *operands):
    vmem = pl.BlockSpec(memory_space=pltpu.VMEM)
    return pl.pallas_call(
        kernel,
        in_specs=[vmem] * len(operands),
        out_specs=vmem,
        out_shape=pltpu.VMEM(out_shape, BF),
        compiler_params=pltpu.CompilerParams(vmem_limit_bytes=40 * 2**20),
        name=name,
    )(*[pltpu.with_memory_space_constraint(x, pltpu.VMEM) for x in operands])


def exchange(x):
    return lax.all_to_all(x, "eng", split_axis=0, concat_axis=0, tiled=True)


def on_device(g_lesser, g_greater, coulomb, coupling, lag_slots):
    parts = lax.axis_size("eng")
    blocks = lax.axis_size("blk")
    own, _, two, bs, _ = g_lesser.shape
    energies = own * parts
    slab = bs // parts
    norm = energies ** (-0.5)
    fwd_np, inv_np = real_tables(energies)
    fwd = jnp.asarray(fwd_np)
    inv = jnp.asarray(inv_np * np.float32(norm))
    back_ids = (-np.arange(energies)) % energies
    ids = jnp.arange(energies, dtype=jnp.int32)
    cnt = jnp.sum((lag_slots[:, None] == ids[None, :]).astype(F32), axis=0)
    cnt_neg = jnp.sum((lag_slots[:, None] == jnp.asarray(back_ids, jnp.int32)[None, :]).astype(F32), axis=0)
    lag_tabs = jnp.stack([fwd * cnt[None], jnp.asarray(fwd_np[:, back_ids]) * cnt_neg[None]])

    both = jnp.stack([g_lesser[:, 0], g_greater[:, 0]], axis=1)
    both = both.reshape(own, 2, two, parts, slab, bs).transpose(3, 0, 1, 2, 4, 5)
    el = exchange(both).reshape(energies, 2 * two * slab * bs)
    columns = two * slab * bs
    c = local_call(corr_kernel, (energies, columns), "corr", fwd, inv, el)

    row = lax.axis_index("blk")
    kept = (coupling[0] * (row < blocks - 1).astype(jnp.int32)).astype(BF)
    v_both = jnp.stack([coulomb[0, 0], coulomb[0, 1] * kept], axis=0)
    v_both = v_both.reshape(two, parts, 1, slab, bs).transpose(1, 2, 0, 3, 4)
    p = exchange(c.reshape(parts, own, two, slab, bs))
    stack = jnp.concatenate([p, v_both], axis=1)
    ups = [(i, i + 1) for i in range(blocks - 1)]
    before = lax.ppermute(stack, "blk", ups)
    after = lax.ppermute(stack, "blk", [(j, i) for i, j in ups])
    w = local_call(screen_kernel, p.shape, "screen", before, stack, after)

    d = exchange(w).reshape(energies, columns)
    s = local_call(conv_kernel, el.shape, "conv", fwd, lag_tabs, inv, el, d)
    s = exchange(s.reshape(parts, own, 2, two, slab, bs))
    s = s.transpose(1, 2, 3, 0, 4, 5).reshape(own, 2, 1, two, bs, bs)
    return (s[:, 0], s[:, 1])


def solution(mesh):
    spec = P("eng", "blk", None, None, None)
    return jax.shard_map(
        on_device,
        mesh=mesh,
        in_specs=(spec, spec, P("blk", None, None, None), P("blk"), P()),
        out_specs=(spec, spec),
        check_vma=False,
    )
```

time: 240 us -> 227 us (0.946)
  Pallas kernels: 18.7 us -> 7.44 us
    pallas_call x3, Pallas kernels: 18.7 us -> 7.44 us  [local_call(): pl.pallas_call(kernel, in_specs=[vmem] * len(operands), out_specs=vmem, o...]
    unnamed x16 -> x14, local copies, waits for them, and re-layouts: 4.66 us -> 1.8 us
where the time goes in v2:
time: 227 us; the launch traced here: 224 us
  blocking collectives  118 us (52%)
  waiting for transfers between devices  69.3 us (31%)
  starting transfers between devices  18 us (8%)
  local copies, waits for them, and re-layouts  8.21 us (4%)
  Pallas kernels  7.44 us (3%)
    all_to_all x2, blocking collectives, exchange(): return lax.all_to_all(x, 'eng', split_axis=0, concat_axis=0, tiled=True)  118 us
    all_to_all x2, waiting for transfers between devices, exchange(): return lax.all_to_all(x, 'eng', split_axis=0, concat_axis=0, tiled=True)  54.2 us
    ppermute x1, waiting for transfers between devices, on_device(): before = lax.ppermute(stack, 'blk', ups)  13.3 us
    all_to_all x2, starting transfers between devices, exchange(): return lax.all_to_all(x, 'eng', split_axis=0, concat_axis=0, tiled=True)  12.4 us
    pallas_call x3, Pallas kernels, local_call(): pl.pallas_call(kernel, in_specs=[vmem] * len(operands), out_specs=vmem, o...  7.44 us
  transfers between devices with their start and end apart: 4, of which 4 were waited for; matrix products, arithmetic and copies ran while one was open for 0% of the time, Pallas kernels for 0%

profile of v2, /device:TPU:66, one launch (start us, length us, event | category | flops | bytes accessed | tf_op | source)
XLA Modules:
  0.0 224.5 jit_solution(14088070731273920606)
XLA Ops:
  0.6 1.7 pad_maximum_fusion
  2.4 0.3 copy.18
  2.7 61.3 %all_to_all.20 = bf16[16,4,2,2,16,256]{5,4,3,2,1,0:T(8,128)(2,1)} all-to-all(bf16[16,4,2,2,16,256]{5,4,3,2,1,0:T(8,128)(2,1)S(1)} %bitcast.33), channel_id=1, replica_groups=mesh['blk'=16,'eng'=16] {'eng'}, dimensions={0} | all-to-all | bytes 4194304 | tf_op jit(solution)/shard_map/all_to_all | solution.py:135
  64.0 2.9 %reshape.44.x_ref.g_ref = bf16[64,16384]{1,0:T(8,128)(2,1)S(1)} reshape(bf16[16,4,2,2,16,256]{5,4,3,2,1,0:T(8,128)(2,1)} %all_to_all.20) | data formatting | bytes 4194304 | tf_op jit(solution)/shard_map/reshape | solution.py:156
  66.9 1.5 corr.1
  68.4 0.0 copy-start.2
  68.4 1.2 copy.15
  69.6 5.5 %all-to-all-start.1 = ((bf16[16,4,2,16,256]{4,3,2,1,0:T(8,128)(2,1)}), bf16[16,4,2,16,256]{4,3,2,1,0:T(8,128)(2,1)S(1)}, u32[]{:S(2)}, u32[]{:S(2)}) async-start(bf16[16,4,2,16,256]{4,3,2,1,0:T(8,128)(2,1)} %bitcast.37), calls=%async_computation.1 | async-start | bytes 2097152 | tf_op jit(solution)/shard_map/all_to_all | solution.py:135
  75.8 26.1 %all-to-all-done.1 = bf16[16,4,2,16,256]{4,3,2,1,0:T(8,128)(2,1)S(1)} async-done(((bf16[16,4,2,16,256]{4,3,2,1,0:T(8,128)(2,1)}), bf16[16,4,2,16,256]{4,3,2,1,0:T(8,128)(2,1)S(1)}, u32[]{:S(2)}, u32[]{:S(2)}) %all-to-all-start.1) | async-done | bytes 1048608 | tf_op jit(solution)/shard_map/all_to_all | solution.py:135
  102.0 0.1 pad_maximum_fusion.1.z_ref
  102.1 1.9 collective-permute-start
  104.0 3.6 %collective-permute-start.1 = (bf16[16,5,2,16,256]{4,3,2,1,0:T(8,128)(2,1)S(1)}, bf16[16,5,2,16,256]{4,3,2,1,0:T(8,128)(2,1)S(1)}, u32[]{:S(2)}, u32[]{:S(2)}) collective-permute-start(bf16[16,5,2,16,256]{4,3,2,1,0:T(8,128)(2,1)S(1)} %pad_maximum_fusion.1.z_ref), channel_id=1, source_target_pairs={{16,0},{32,16},{48,32},{64,48},{80,64},{96,80},{112,96},{128,112},... | collective-permute-start | bytes 3932168 | tf_op jit(solution)/shard_map/ppermute | solution.py:168
  107.7 13.3 %collective-permute-done.m_ref = bf16[16,5,2,16,256]{4,3,2,1,0:T(8,128)(2,1)S(1)} collective-permute-done((bf16[16,5,2,16,256]{4,3,2,1,0:T(8,128)(2,1)S(1)}, bf16[16,5,2,16,256]{4,3,2,1,0:T(8,128)(2,1)S(1)}, u32[]{:S(2)}, u32[]{:S(2)}) %collective-permute-start) | collective-permute-done | bytes 1310752 | tf_op jit(solution)/shard_map/ppermute | solution.py:167
  121.0 1.8 collective-permute-done.1.p_ref
  122.8 3.1 %screen.1 = bf16[16,4,2,16,256]{4,3,2,1,0:T(8,128)(2,1)} custom-call(bf16[16,5,2,16,256]{4,3,2,1,0:T(8,128)(2,1)S(1)} %collective-permute-done.m_ref, bf16[16,5,2,16,256]{4,3,2,1,0:T(8,128)(2,1)S(1)} %pad_maximum_fusion.1.z_ref, bf16[16,5,2,16,256]{4,3,2,1,0:T(8,128)(2,1)S(1)} %collective-permute-done.1.p_ref), custom_call_target="tpu_custom_call" | custom-call | tf_op jit(solution)/shard_map/screen/pallas_call | solution.py:124
  125.9 6.9 %all-to-all-start.2 = ((bf16[16,4,2,16,256]{4,3,2,1,0:T(8,128)(2,1)}), bf16[16,4,2,16,256]{4,3,2,1,0:T(8,128)(2,1)}, u32[]{:S(2)}, u32[]{:S(2)}) async-start(bf16[16,4,2,16,256]{4,3,2,1,0:T(8,128)(2,1)} %screen.1), calls=%async_computation.2 | async-start | bytes 2097152 | tf_op jit(solution)/shard_map/all_to_all | solution.py:135
  132.8 0.1 convert_reduce_fusion.1
  132.9 28.0 %all-to-all-done.2 = bf16[16,4,2,16,256]{4,3,2,1,0:T(8,128)(2,1)} async-done(((bf16[16,4,2,16,256]{4,3,2,1,0:T(8,128)(2,1)}), bf16[16,4,2,16,256]{4,3,2,1,0:T(8,128)(2,1)}, u32[]{:S(2)}, u32[]{:S(2)}) %all-to-all-start.2) | async-done | bytes 1048608 | tf_op jit(solution)/shard_map/all_to_all | solution.py:135
  161.0 1.6 reshape.46.d_ref
  162.5 2.8 %conv.1 = bf16[64,16384]{1,0:T(8,128)(2,1)S(1)} custom-call(f32[64,64]{1,0:T(8,128)S(1)} %copy-done, f32[2,64,64]{2,1,0:T(8,128)S(1)} %pad_maximum_fusion.2.lag_ref, f32[64,64]{1,0:T(8,128)S(1)} %copy-done.1, bf16[64,16384]{1,0:T(8,128)(2,1)S(1)} %reshape.44.x_ref.g_ref, bf16[64,8192]{1,0:T(8,128)(2,1)S(1)} %reshape.46.d_ref), custom_call_target="tpu_custom_call" | custom-call | tf_op jit(solution)/shard_map/conv/pallas_call | solution.py:124
  165.4 0.5 copy.16
  165.9 56.9 %all_to_all.21 = bf16[16,4,2,2,16,256]{5,4,3,2,1,0:T(8,128)(2,1)S(1)} all-to-all(bf16[16,4,2,2,16,256]{5,4,3,2,1,0:T(8,128)(2,1)S(1)} %bitcast.34), channel_id=1, replica_groups=mesh['blk'=16,'eng'=16] {'eng'}, dimensions={0} | all-to-all | bytes 4194304 | tf_op jit(solution)/shard_map/all_to_all | solution.py:135
  222.8 0.2 copy.14
  223.0 1.5 slice_bitcast_fusion
  (15 shorter events, 0.1 us)
Async XLA Ops:
  64.0 2.9 %copy-start = (f32[64,64]{1,0:T(8,128)S(1)}, f32[64,64]{1,0:T(8,128)}, u32[]{:S(2)}) copy-start(f32[64,64]{1,0:T(8,128)} %constant.19.clone.fwd_ref) | copy-start | bytes 49156
  64.0 2.9 %copy-start.1 = (f32[64,64]{1,0:T(8,128)S(1)}, f32[64,64]{1,0:T(8,128)}, u32[]{:S(2)}) copy-start(f32[64,64]{1,0:T(8,128)} %constant.20.clone.inv_ref) | copy-start | bytes 49156
  68.4 7.4 %copy-start.2 = (bf16[1,2,256,256]{3,2,1,0:T(8,128)(2,1)S(1)}, bf16[1,2,256,256]{3,2,1,0:T(8,128)(2,1)}, u32[]{:S(2)}) copy-start(bf16[1,2,256,256]{3,2,1,0:T(8,128)(2,1)} %param.11) | copy-start | bytes 786436
  69.6 32.3 %all-to-all-start.1 = ((bf16[16,4,2,16,256]{4,3,2,1,0:T(8,128)(2,1)}), bf16[16,4,2,16,256]{4,3,2,1,0:T(8,128)(2,1)S(1)}, u32[]{:S(2)}, u32[]{:S(2)}) async-start(bf16[16,4,2,16,256]{4,3,2,1,0:T(8,128)(2,1)} %bitcast.37), calls=%async_computation.1 | async-start | bytes 2097152 | tf_op jit(solution)/shard_map/all_to_all | solution.py:135
  102.1 18.9 %collective-permute-start = (bf16[16,5,2,16,256]{4,3,2,1,0:T(8,128)(2,1)S(1)}, bf16[16,5,2,16,256]{4,3,2,1,0:T(8,128)(2,1)S(1)}, u32[]{:S(2)}, u32[]{:S(2)}) collective-permute-start(bf16[16,5,2,16,256]{4,3,2,1,0:T(8,128)(2,1)S(1)} %pad_maximum_fusion.1.z_ref), channel_id=1, source_target_pairs={{0,16},{16,32},{32,48},{48,64},{64,80},{80,96},{96,112},{112,128},... | collective-permute-start | bytes 3932168 | tf_op jit(solution)/shard_map/ppermute | solution.py:167
  104.0 18.8 %collective-permute-start.1 = (bf16[16,5,2,16,256]{4,3,2,1,0:T(8,128)(2,1)S(1)}, bf16[16,5,2,16,256]{4,3,2,1,0:T(8,128)(2,1)S(1)}, u32[]{:S(2)}, u32[]{:S(2)}) collective-permute-start(bf16[16,5,2,16,256]{4,3,2,1,0:T(8,128)(2,1)S(1)} %pad_maximum_fusion.1.z_ref), channel_id=1, source_target_pairs={{16,0},{32,16},{48,32},{64,48},{80,64},{96,80},{112,96},{128,112},... | collective-permute-start | bytes 3932168 | tf_op jit(solution)/shard_map/ppermute | solution.py:168
  125.9 6.9 %copy-start.4 = (s32[64]{0:T(128)S(1)}, s32[64]{0:T(128)}, u32[]{:S(2)}) copy-start(s32[64]{0:T(128)} %param.13) | copy-start | bytes 772
  125.9 6.9 %copy-start.5 = (s32[64]{0:T(128)S(1)}, s32[64]{0:T(128)}, u32[]{:S(2)}) copy-start(s32[64]{0:T(128)} %constant.21.clone) | copy-start | bytes 772
  125.9 7.0 %copy-start.3 = (f32[64,64]{1,0:T(8,128)S(1)}, f32[64,64]{1,0:T(8,128)}, u32[]{:S(2)}) copy-start(f32[64,64]{1,0:T(8,128)} %constant.22.clone) | copy-start | bytes 49156
  125.9 35.1 %all-to-all-start.2 = ((bf16[16,4,2,16,256]{4,3,2,1,0:T(8,128)(2,1)}), bf16[16,4,2,16,256]{4,3,2,1,0:T(8,128)(2,1)}, u32[]{:S(2)}, u32[]{:S(2)}) async-start(bf16[16,4,2,16,256]{4,3,2,1,0:T(8,128)(2,1)} %screen.1), calls=%async_computation.2 | async-start | bytes 2097152 | tf_op jit(solution)/shard_map/all_to_all | solution.py:135

commit v3 on v2

--- a/solution.py
+++ b/solution.py
@@ -8,6 +8,10 @@
 
 BF = jnp.bfloat16
 F32 = jnp.float32
+MIB = 2**20
+
+FIRST = 20000
+SECOND = 10000
 
 
 def real_tables(n):
@@ -87,6 +91,7 @@
 
 def screen_kernel(m_ref, z_ref, p_ref, w_ref):
     own = w_ref.shape[1]
+    take_turn(SECOND)
 
     def block(ref, k, j):
         x = ref[:, k, j]
@@ -119,16 +124,93 @@
         w_ref[:, k, 1] = w_up.astype(w_ref.dtype).reshape(shape)
 
 
-def local_call(kernel, out_shape, name, *operands):
-    vmem = pl.BlockSpec(memory_space=pltpu.VMEM)
+VMEM = pl.BlockSpec(memory_space=pltpu.VMEM)
+HBM = pl.BlockSpec(memory_space=pltpu.HBM)
+
+
+def local_call(kernel, out_shape, name, *operands, near=True, mib=32):
     return pl.pallas_call(
         kernel,
-        in_specs=[vmem] * len(operands),
-        out_specs=vmem,
-        out_shape=pltpu.VMEM(out_shape, BF),
-        compiler_params=pltpu.CompilerParams(vmem_limit_bytes=40 * 2**20),
+        in_specs=[VMEM] * len(operands),
+        out_specs=VMEM if near else VMEM,
+        out_shape=pltpu.VMEM(out_shape, BF) if near else jax.ShapeDtypeStruct(out_shape, BF),
+        compiler_params=pltpu.CompilerParams(vmem_limit_bytes=mib * MIB),
         name=name,
     )(*[pltpu.with_memory_space_constraint(x, pltpu.VMEM) for x in operands])
+
+
+def far(x):
+    return pltpu.with_memory_space_constraint(x, pltpu.HBM)
+
+
+def take_turn(nanos):
+    @pl.when(lax.axis_index("blk") % 2 == 1)
+    def _():
+        pl.delay(nanos)
+
+
+def run_all(copies):
+    for c in copies:
+        c.start()
+    return copies
+
+
+def pack_kernel(l_ref, g_ref, o_ref, sems):
+    parts, slab = o_ref.shape[0], o_ref.shape[4]
+    copies = run_all(
+        [
+            pltpu.make_async_copy(
+                ref.at[:, 0, :, pl.ds(q * slab, slab), :], o_ref.at[q, :, kind], sems.at[kind, q]
+            )
+            for q in range(parts)
+            for kind, ref in enumerate((l_ref, g_ref))
+        ]
+    )
+    take_turn(FIRST)
+    for c in copies:
+        c.wait()
+
+
+def pack(g_lesser, g_greater, parts):
+    own, _, two, bs, _ = g_lesser.shape
+    return pl.pallas_call(
+        pack_kernel,
+        in_specs=[HBM, HBM],
+        out_specs=VMEM,
+        out_shape=pltpu.VMEM((parts, own, 2, two, bs // parts, bs), BF),
+        scratch_shapes=[pltpu.SemaphoreType.DMA((2, parts))],
+        compiler_params=pltpu.CompilerParams(vmem_limit_bytes=8 * MIB),
+        name="pack",
+    )(far(g_lesser), far(g_greater))
+
+
+def unpack_kernel(s_ref, l_ref, g_ref, sems):
+    parts, slab = s_ref.shape[0], s_ref.shape[4]
+    copies = run_all(
+        [
+            pltpu.make_async_copy(
+                s_ref.at[q, :, kind], ref.at[:, 0, :, pl.ds(q * slab, slab), :], sems.at[kind, q]
+            )
+            for q in range(parts)
+            for kind, ref in enumerate((l_ref, g_ref))
+        ]
+    )
+    for c in copies:
+        c.wait()
+
+
+def unpack(s):
+    parts, own, _, two, slab, bs = s.shape
+    out = jax.ShapeDtypeStruct((own, 1, two, bs, bs), BF)
+    return pl.pallas_call(
+        unpack_kernel,
+        in_specs=[VMEM],
+        out_specs=[HBM, HBM],
+        out_shape=[out, out],
+        scratch_shapes=[pltpu.SemaphoreType.DMA((2, parts))],
+        compiler_params=pltpu.CompilerParams(vmem_limit_bytes=8 * MIB),
+        name="unpack",
+    )(pltpu.with_memory_space_constraint(s, pltpu.VMEM))
 
 
 def exchange(x):
@@ -151,13 +233,11 @@
     cnt_neg = jnp.sum((lag_slots[:, None] == jnp.asarray(back_ids, jnp.int32)[None, :]).astype(F32), axis=0)
     lag_tabs = jnp.stack([fwd * cnt[None], jnp.asarray(fwd_np[:, back_ids]) * cnt_neg[None]])
 
-    both = jnp.stack([g_lesser[:, 0], g_greater[:, 0]], axis=1)
-    both = both.reshape(own, 2, two, parts, slab, bs).transpose(3, 0, 1, 2, 4, 5)
-    el = exchange(both).reshape(energies, 2 * two * slab * bs)
+    row = lax.axis_index("blk")
+    el = exchange(pack(g_lesser, g_greater, parts)).reshape(energies, 2 * two * slab * bs)
     columns = two * slab * bs
     c = local_call(corr_kernel, (energies, columns), "corr", fwd, inv, el)
 
-    row = lax.axis_index("blk")
     kept = (coupling[0] * (row < blocks - 1).astype(jnp.int32)).astype(BF)
     v_both = jnp.stack([coulomb[0, 0], coulomb[0, 1] * kept], axis=0)
     v_both = v_both.reshape(two, parts, 1, slab, bs).transpose(1, 2, 0, 3, 4)
@@ -166,13 +246,12 @@
     ups = [(i, i + 1) for i in range(blocks - 1)]
     before = lax.ppermute(stack, "blk", ups)
     after = lax.ppermute(stack, "blk", [(j, i) for i, j in ups])
-    w = local_call(screen_kernel, p.shape, "screen", before, stack, after)
+    w = local_call(screen_kernel, p.shape, "screen", before, stack, after, near=False, mib=24)
 
     d = exchange(w).reshape(energies, columns)
     s = local_call(conv_kernel, el.shape, "conv", fwd, lag_tabs, inv, el, d)
     s = exchange(s.reshape(parts, own, 2, two, slab, bs))
-    s = s.transpose(1, 2, 3, 0, 4, 5).reshape(own, 2, 1, two, bs, bs)
-    return (s[:, 0], s[:, 1])
+    return tuple(unpack(s))
 
 
 def solution(mesh):

time: 227 us -> 217 us (0.956)
  the two profiles are of different devices: /device:TPU:66 before, /device:TPU:1 now
where the time goes in v3:
time: 217 us; the launch traced here: 216 us
  blocking collectives  85.5 us (39%)
  waiting for transfers between devices  66.6 us (31%)
  Pallas kernels  39.5 us (18%)
  starting transfers between devices  16.5 us (8%)
  local copies, waits for them, and re-layouts  6.23 us (3%)
    all_to_all x2, blocking collectives, exchange(): return lax.all_to_all(x, 'eng', split_axis=0, concat_axis=0, tiled=True)  85.5 us
    all_to_all x2, waiting for transfers between devices, exchange(): return lax.all_to_all(x, 'eng', split_axis=0, concat_axis=0, tiled=True)  49.8 us
    pallas_call x1, Pallas kernels, pack(): pl.pallas_call(pack_kernel, in_specs=[HBM, HBM], out_specs=VMEM, out_shap...  20.5 us
    pallas_call x3, Pallas kernels, local_call(): pl.pallas_call(kernel, in_specs=[VMEM] * len(operands), out_specs=VMEM if...  17.4 us
    all_to_all x2, starting transfers between devices, exchange(): return lax.all_to_all(x, 'eng', split_axis=0, concat_axis=0, tiled=True)  12.1 us
    ppermute x1, waiting for transfers between devices, on_device(): before = lax.ppermute(stack, 'blk', ups)  12 us
    ppermute x1, waiting for transfers between devices, on_device(): after = lax.ppermute(stack, 'blk', [(j, i) for i, j in ups])  4.8 us
  transfers between devices with their start and end apart: 4, of which 4 were waited for; matrix products, arithmetic and copies ran while one was open for 0% of the time, Pallas kernels for 0%

profile of v3, /device:TPU:1, one launch (start us, length us, event | category | flops | bytes accessed | tf_op | source)
XLA Modules:
  0.0 216.1 jit_solution(7674859414030698758)
XLA Ops:
  0.6 20.5 %pack.1 = bf16[16,4,2,2,16,256]{5,4,3,2,1,0:T(8,128)(2,1)S(1)} custom-call(bf16[4,1,2,256,256]{4,3,2,1,0:T(8,128)(2,1)} %l_ref.1, bf16[4,1,2,256,256]{4,3,2,1,0:T(8,128)(2,1)} %g_ref.1), custom_call_target="tpu_custom_call" | custom-call | tf_op jit(solution)/shard_map/pack/pallas_call | solution.py:176
  21.1 44.8 %all_to_all.20 = bf16[16,4,2,2,16,256]{5,4,3,2,1,0:T(8,128)(2,1)} all-to-all(bf16[16,4,2,2,16,256]{5,4,3,2,1,0:T(8,128)(2,1)S(1)} %pack.1), channel_id=1, replica_groups=mesh['blk'=16,'eng'=16] {'eng'}, dimensions={0} | all-to-all | bytes 4194304 | tf_op jit(solution)/shard_map/all_to_all | solution.py:217
  65.9 2.9 %reshape.37.x_ref.g_ref = bf16[64,16384]{1,0:T(8,128)(2,1)S(1)} reshape(bf16[16,4,2,2,16,256]{5,4,3,2,1,0:T(8,128)(2,1)} %all_to_all.20) | data formatting | bytes 4194304 | tf_op jit(solution)/shard_map/reshape | solution.py:237
  68.8 0.0 copy-done
  68.8 1.5 corr.1
  70.3 0.0 copy-start.2
  70.3 1.2 copy.11
  71.6 5.8 %all-to-all-start.1 = ((bf16[16,4,2,16,256]{4,3,2,1,0:T(8,128)(2,1)}), bf16[16,4,2,16,256]{4,3,2,1,0:T(8,128)(2,1)S(1)}, u32[]{:S(2)}, u32[]{:S(2)}) async-start(bf16[16,4,2,16,256]{4,3,2,1,0:T(8,128)(2,1)} %bitcast.23), calls=%async_computation.1 | async-start | bytes 2097152 | tf_op jit(solution)/shard_map/all_to_all | solution.py:217
  78.1 0.0 copy-done.2
  78.1 26.6 %all-to-all-done.1 = bf16[16,4,2,16,256]{4,3,2,1,0:T(8,128)(2,1)S(1)} async-done(((bf16[16,4,2,16,256]{4,3,2,1,0:T(8,128)(2,1)}), bf16[16,4,2,16,256]{4,3,2,1,0:T(8,128)(2,1)S(1)}, u32[]{:S(2)}, u32[]{:S(2)}) %all-to-all-start.1) | async-done | bytes 1048608 | tf_op jit(solution)/shard_map/all_to_all | solution.py:217
  104.8 0.1 pad_maximum_fusion.z_ref
  104.9 1.9 collective-permute-start
  106.8 2.5 %collective-permute-start.1 = (bf16[16,5,2,16,256]{4,3,2,1,0:T(8,128)(2,1)S(1)}, bf16[16,5,2,16,256]{4,3,2,1,0:T(8,128)(2,1)S(1)}, u32[]{:S(2)}, u32[]{:S(2)}) collective-permute-start(bf16[16,5,2,16,256]{4,3,2,1,0:T(8,128)(2,1)S(1)} %pad_maximum_fusion.z_ref), channel_id=1, source_target_pairs={{16,0},{32,16},{48,32},{64,48},{80,64},{96,80},{112,96},{128,112},... | collective-permute-start | bytes 3932168 | tf_op jit(solution)/shard_map/ppermute | solution.py:248
  109.3 12.0 %collective-permute-done.m_ref = bf16[16,5,2,16,256]{4,3,2,1,0:T(8,128)(2,1)S(1)} collective-permute-done((bf16[16,5,2,16,256]{4,3,2,1,0:T(8,128)(2,1)S(1)}, bf16[16,5,2,16,256]{4,3,2,1,0:T(8,128)(2,1)S(1)}, u32[]{:S(2)}, u32[]{:S(2)}) %collective-permute-start) | collective-permute-done | bytes 1310752 | tf_op jit(solution)/shard_map/ppermute | solution.py:247
  121.3 4.8 %collective-permute-done.1.p_ref = bf16[16,5,2,16,256]{4,3,2,1,0:T(8,128)(2,1)S(1)} collective-permute-done((bf16[16,5,2,16,256]{4,3,2,1,0:T(8,128)(2,1)S(1)}, bf16[16,5,2,16,256]{4,3,2,1,0:T(8,128)(2,1)S(1)}, u32[]{:S(2)}, u32[]{:S(2)}) %collective-permute-start.1) | collective-permute-done | bytes 1310752 | tf_op jit(solution)/shard_map/ppermute | solution.py:248
  126.1 13.1 %screen.1 = bf16[16,4,2,16,256]{4,3,2,1,0:T(8,128)(2,1)} custom-call(bf16[16,5,2,16,256]{4,3,2,1,0:T(8,128)(2,1)S(1)} %collective-permute-done.m_ref, bf16[16,5,2,16,256]{4,3,2,1,0:T(8,128)(2,1)S(1)} %pad_maximum_fusion.z_ref, bf16[16,5,2,16,256]{4,3,2,1,0:T(8,128)(2,1)S(1)} %collective-permute-done.1.p_ref), custom_call_target="tpu_custom_call" | custom-call | tf_op jit(solution)/shard_map/screen/pallas_call | solution.py:132
  139.2 6.3 %all-to-all-start.2 = ((bf16[16,4,2,16,256]{4,3,2,1,0:T(8,128)(2,1)}), bf16[16,4,2,16,256]{4,3,2,1,0:T(8,128)(2,1)}, u32[]{:S(2)}, u32[]{:S(2)}) async-start(bf16[16,4,2,16,256]{4,3,2,1,0:T(8,128)(2,1)} %screen.1), calls=%async_computation.2 | async-start | bytes 2097152 | tf_op jit(solution)/shard_map/all_to_all | solution.py:217
  145.5 0.1 convert_reduce_fusion.1
  145.6 23.2 %all-to-all-done.2 = bf16[16,4,2,16,256]{4,3,2,1,0:T(8,128)(2,1)} async-done(((bf16[16,4,2,16,256]{4,3,2,1,0:T(8,128)(2,1)}), bf16[16,4,2,16,256]{4,3,2,1,0:T(8,128)(2,1)}, u32[]{:S(2)}, u32[]{:S(2)}) %all-to-all-start.2) | async-done | bytes 1048608 | tf_op jit(solution)/shard_map/all_to_all | solution.py:217
  168.8 1.6 reshape.39.d_ref
  170.4 2.9 %conv.1 = bf16[64,16384]{1,0:T(8,128)(2,1)S(1)} custom-call(f32[64,64]{1,0:T(8,128)S(1)} %copy-done, f32[2,64,64]{2,1,0:T(8,128)S(1)} %pad_maximum_fusion.1.lag_ref, f32[64,64]{1,0:T(8,128)S(1)} %copy-done.1, bf16[64,16384]{1,0:T(8,128)(2,1)S(1)} %reshape.37.x_ref.g_ref, bf16[64,8192]{1,0:T(8,128)(2,1)S(1)} %reshape.39.d_ref), custom_call_target="tpu_custom_call" | custom-call | tf_op jit(solution)/shard_map/conv/pallas_call | solution.py:132
  173.2 0.5 copy.12
  173.8 40.7 %all_to_all.21.s_ref = bf16[16,4,2,2,16,256]{5,4,3,2,1,0:T(8,128)(2,1)S(1)} all-to-all(bf16[16,4,2,2,16,256]{5,4,3,2,1,0:T(8,128)(2,1)S(1)} %bitcast.22), channel_id=1, replica_groups=mesh['blk'=16,'eng'=16] {'eng'}, dimensions={0} | all-to-all | bytes 4194304 | tf_op jit(solution)/shard_map/all_to_all | solution.py:217
  214.5 1.6 unpack.1
  (13 shorter events, 0.1 us)
Async XLA Ops:
  65.9 2.9 %copy-start = (f32[64,64]{1,0:T(8,128)S(1)}, f32[64,64]{1,0:T(8,128)}, u32[]{:S(2)}) copy-start(f32[64,64]{1,0:T(8,128)} %constant.19.clone.fwd_ref) | copy-start | bytes 49156
  65.9 2.9 %copy-start.1 = (f32[64,64]{1,0:T(8,128)S(1)}, f32[64,64]{1,0:T(8,128)}, u32[]{:S(2)}) copy-start(f32[64,64]{1,0:T(8,128)} %constant.20.clone.inv_ref) | copy-start | bytes 49156
  70.3 7.8 %copy-start.2 = (bf16[1,2,256,256]{3,2,1,0:T(8,128)(2,1)S(1)}, bf16[1,2,256,256]{3,2,1,0:T(8,128)(2,1)}, u32[]{:S(2)}) copy-start(bf16[1,2,256,256]{3,2,1,0:T(8,128)(2,1)} %param.11) | copy-start | bytes 786436
  71.6 33.2 %all-to-all-start.1 = ((bf16[16,4,2,16,256]{4,3,2,1,0:T(8,128)(2,1)}), bf16[16,4,2,16,256]{4,3,2,1,0:T(8,128)(2,1)S(1)}, u32[]{:S(2)}, u32[]{:S(2)}) async-start(bf16[16,4,2,16,256]{4,3,2,1,0:T(8,128)(2,1)} %bitcast.23), calls=%async_computation.1 | async-start | bytes 2097152 | tf_op jit(solution)/shard_map/all_to_all | solution.py:217
  104.9 16.5 %collective-permute-start = (bf16[16,5,2,16,256]{4,3,2,1,0:T(8,128)(2,1)S(1)}, bf16[16,5,2,16,256]{4,3,2,1,0:T(8,128)(2,1)S(1)}, u32[]{:S(2)}, u32[]{:S(2)}) collective-permute-start(bf16[16,5,2,16,256]{4,3,2,1,0:T(8,128)(2,1)S(1)} %pad_maximum_fusion.z_ref), channel_id=1, source_target_pairs={{0,16},{16,32},{32,48},{48,64},{64,80},{80,96},{96,112},{112,128},... | collective-permute-start | bytes 3932168 | tf_op jit(solution)/shard_map/ppermute | solution.py:247
  106.8 19.3 %collective-permute-start.1 = (bf16[16,5,2,16,256]{4,3,2,1,0:T(8,128)(2,1)S(1)}, bf16[16,5,2,16,256]{4,3,2,1,0:T(8,128)(2,1)S(1)}, u32[]{:S(2)}, u32[]{:S(2)}) collective-permute-start(bf16[16,5,2,16,256]{4,3,2,1,0:T(8,128)(2,1)S(1)} %pad_maximum_fusion.z_ref), channel_id=1, source_target_pairs={{16,0},{32,16},{48,32},{64,48},{80,64},{96,80},{112,96},{128,112},... | collective-permute-start | bytes 3932168 | tf_op jit(solution)/shard_map/ppermute | solution.py:248
  139.2 6.3 %copy-start.4 = (s32[64]{0:T(128)S(1)}, s32[64]{0:T(128)}, u32[]{:S(2)}) copy-start(s32[64]{0:T(128)} %param.13) | copy-start | bytes 772
  139.2 6.3 %copy-start.5 = (s32[64]{0:T(128)S(1)}, s32[64]{0:T(128)}, u32[]{:S(2)}) copy-start(s32[64]{0:T(128)} %constant.21.clone) | copy-start | bytes 772
  139.2 6.4 %copy-start.3 = (f32[64,64]{1,0:T(8,128)S(1)}, f32[64,64]{1,0:T(8,128)}, u32[]{:S(2)}) copy-start(f32[64,64]{1,0:T(8,128)} %constant.22.clone) | copy-start | bytes 49156
  139.2 29.6 %all-to-all-start.2 = ((bf16[16,4,2,16,256]{4,3,2,1,0:T(8,128)(2,1)}), bf16[16,4,2,16,256]{4,3,2,1,0:T(8,128)(2,1)}, u32[]{:S(2)}, u32[]{:S(2)}) async-start(bf16[16,4,2,16,256]{4,3,2,1,0:T(8,128)(2,1)} %screen.1), calls=%async_computation.2 | async-start | bytes 2097152 | tf_op jit(solution)/shard_map/all_to_all | solution.py:217
